TPU v7x, 256 devices: a whole 4x4x8 slice. The times are simulated.
256 devices in a mesh: grp: 8 (over z), feat: 32 (over x, y, core).
Axes of the slice: x: 4, y: 4, z: 8, core: 2. Of those that a mesh axis runs over, the one named last changes fastest.
Arguments:
- features: bfloat16 [65536, 512], P(('grp', 'feat')), may hold values from -6 to 6
- adj_tiles: bfloat16 [512, 16, 128, 128], P(('grp', 'feat')), may hold values from 0.0099487305 to 1
- src_block: int32 [512, 16], P(('grp', 'feat')), may hold values from 0 to 63, as said below
- counts: int32 [512], P(('grp', 'feat')), may hold values from 1 to 16, as said below
- w_self: bfloat16 [512, 512], replicated, may hold values from -0.25 to 0.25
- w_neigh: bfloat16 [512, 512], replicated, may hold values from -0.25 to 0.25
- multiplier: float32 [512], replicated, may hold values from 0.5 to 2
- bit_shift: int32 [512], replicated, may hold values from 0 to 2
- cotangent: bfloat16 [65536, 512], P(('grp', 'feat')), may hold values from -6 to 6
Outputs:
- output: bfloat16 [65536, 512], P(('grp', 'feat'))
- grad_features: bfloat16 [65536, 512], P(('grp', 'feat'))
- grad_self: float32 [512, 512], replicated
- grad_neigh: float32 [512, 512], replicated
Inputs may be any that keep to these rules, and one draw needn't show every extreme that they name: src_block[i, k] is a block of block i's own group, held by a device at most 2 positions from block i's device in the group's cyclic order of devices (block i is held by device (i % 64) // 2 of its group, which holds 2 consecutive blocks); the distance 2 is reached in both directions in every draw. Slots k >= counts[i] take no part.
All inputs are finite; a program needn't handle non-finite values.
Results may differ from a plain program's by a relative error of at most 0.0059.
Values may be sent and summed in bfloat16 or wider, within the bound.
No kernel may reach another device: no remote copies, remote signals or barrier semaphores. Data moves between devices by JAX's collectives and lax.ppermute only.
A program may use at most 64 MiB of HBM per device.

v0:
```python
import math
import jax
import jax.numpy as jnp
from jax import lax
from jax.sharding import PartitionSpec as P

SPAN = 2


def passed_along(x, axis, by):
    peers = lax.axis_size(axis)
    return lax.ppermute(x, axis, [(i, (i + by) % peers) for i in range(peers)])


def fetch_near(shard_piece, steps_by):
    return passed_along(shard_piece, "feat", steps_by)


def return_near(shard_piece, steps_by):
    return passed_along(shard_piece, "feat", steps_by)


def local(
    features, adj_tiles, src_block, counts, w_self, w_neigh, multiplier, bit_shift, cotangent
):
    num_blocks = adj_tiles.shape[0]
    num_slots = adj_tiles.shape[1]
    block_len = adj_tiles.shape[2]
    feature_width = features.shape[1]
    row_count = features.shape[0]
    feat_count = lax.axis_size("feat")
    my_index = lax.axis_index("feat")
    live_mask = jnp.arange(num_slots, dtype=jnp.int32)[None, :] < counts[:, None]
    masked = jnp.where(live_mask[:, :, None, None], adj_tiles, jnp.zeros_like(adj_tiles))
    degree = jnp.sum(masked, axis=(1, 3), dtype=jnp.float32)
    inv_root = lax.rsqrt(degree)
    node_blocks = features.reshape(num_blocks, block_len, feature_width)
    pieces = {0: node_blocks}
    for offset in range(-SPAN, SPAN + 1):
        if offset != 0:
            pieces[offset] = fetch_near(node_blocks, -offset)
    source_pool = jnp.concatenate([pieces[offset] for offset in range(-SPAN, SPAN + 1)], axis=0)
    relative = (src_block // num_blocks - my_index + SPAN) % feat_count
    slot_index = relative * num_blocks + src_block % num_blocks
    flat_index = slot_index.reshape(-1)
    sources = jnp.take(source_pool, flat_index, axis=0).reshape(
        num_blocks, num_slots, block_len, feature_width
    )
    summed = jnp.einsum("bkij,bkjf->bif", masked, sources, preferred_element_type=jnp.float32)
    aggregated = (
        (summed * inv_root[:, :, None]).astype(jnp.bfloat16).reshape(row_count, feature_width)
    )
    preact = jnp.dot(features, w_self, preferred_element_type=jnp.float32)
    preact = preact + jnp.dot(aggregated, w_neigh, preferred_element_type=jnp.float32)
    scale = multiplier * jnp.exp2(-bit_shift.astype(jnp.float32))
    scaled = preact * scale
    sigmoid_val = jax.nn.sigmoid(scaled)
    output = (scaled * sigmoid_val).astype(jnp.bfloat16)
    grad_pre = (
        cotangent.astype(jnp.float32) * sigmoid_val * (1.0 + scaled * (1.0 - sigmoid_val)) * scale
    ).astype(jnp.bfloat16)
    part_self = jnp.dot(features.T, grad_pre, preferred_element_type=jnp.float32)
    part_neigh = jnp.dot(aggregated.T, grad_pre, preferred_element_type=jnp.float32)
    total_self, total_neigh = lax.psum((part_self, part_neigh), ("grp", "feat"))
    grad_scale = 1.0 / math.sqrt(row_count * lax.axis_size("grp") * feat_count)
    own_part = jnp.dot(grad_pre, w_self.T, preferred_element_type=jnp.float32)
    back = jnp.dot(grad_pre, w_neigh.T, preferred_element_type=jnp.float32).reshape(
        num_blocks, block_len, feature_width
    )
    back = (back * inv_root[:, :, None]).astype(jnp.bfloat16)
    contrib = jnp.einsum("bkij,bif->bkjf", masked, back, preferred_element_type=jnp.float32)
    contrib_flat = contrib.reshape(num_blocks * num_slots, block_len * feature_width)
    window_count = (2 * SPAN + 1) * num_blocks
    grouped = jax.ops.segment_sum(contrib_flat, flat_index, num_segments=window_count)
    window = lax.optimization_barrier(grouped.astype(jnp.bfloat16))
    window = window.reshape(window_count, block_len, feature_width)

    def window_piece(offset):
        first_block = (offset + SPAN) * num_blocks
        return window[first_block : first_block + num_blocks]

    spread_blocks = window_piece(0).astype(jnp.float32)
    for offset in range(-SPAN, SPAN + 1):
        if offset != 0:
            arrived = return_near(window_piece(offset), offset)
            spread_blocks = spread_blocks + arrived.astype(jnp.float32)
    spread = spread_blocks.reshape(row_count, feature_width)
    grad_features = (own_part + spread).astype(jnp.bfloat16)
    return (output, grad_features, total_self * grad_scale, total_neigh * grad_scale)


def solution(mesh):
    return jax.shard_map(
        local,
        mesh=mesh,
        in_specs=(
            P(("grp", "feat"), None),
            P(("grp", "feat"), None, None, None),
            P(("grp", "feat"), None),
            P(("grp", "feat")),
            P(),
            P(),
            P(),
            P(),
            P(("grp", "feat"), None),
        ),
        out_specs=(P(("grp", "feat"), None), P(("grp", "feat"), None), P(), P()),
        check_vma=False,
    )
```

profile of v0, /device:TPU:2, one launch (start us, length us, event | category | flops | bytes accessed | tf_op | source)
XLA Modules:
  0.0 402.8 jit_solution(4255000697265647718)
XLA Ops:
  7.2 1.7 collective-permute-start
  8.9 3.9 collective-permute-start.2
  12.7 0.5 collective-permute-start.3
  13.2 0.7 compare_and_fusion
  14.0 0.7 iota_compare_fusion
  14.7 2.2 fusion.33
  16.9 0.7 exponential_multiply_fusion
  17.6 1.6 convert_reduce_fusion
  19.4 1.1 collective-permute-done.1
  20.6 1.4 collective-permute-done.3
  22.0 2.8 gather_fusion
  24.8 3.1 fusion.11
  27.9 1.2 multiply_convert_fusion.1
  29.2 1.3 fusion.35
  30.5 1.3 convolution_bitcast_fusion
  32.1 1.4 fusion.14
  33.5 8.1 %copy.21 = f32[4,8,128,512]{3,1,2,0:T(8,128)} copy(f32[4,8,128,512]{3,2,1,0:T(8,128)S(1)} %bitcast.65) | data formatting | bytes 16777216
  41.6 2.2 broadcast_in_dim.35
  43.9 75.4 %scatter_fusion = f32[10,65536]{1,0:T(8,128)} fusion(f32[10,65536]{1,0:T(8,128)} %broadcast_in_dim.35, s32[32]{0:T(128)S(1)} %reshape.113, f32[32,65536]{1,0:T(8,128)} %bitcast.64), kind=kCustom, calls=%fused_computation.1 | custom fusion | flops 2097152 | bytes 25165952 | tf_op jit(solution)/shard_map/scatter-add | solution.py:74
  119.3 2.4 convert_element_type.52
  121.7 0.8 fusion.32
  122.6 4.9 %collective-permute-start.4 = (bf16[2,128,512]{2,1,0:T(8,128)(2,1)S(1)}, bf16[2,128,512]{2,1,0:T(8,128)(2,1)S(1)}, u32[]{:S(2)}, u32[]{:S(2)}) collective-permute-start(bf16[2,128,512]{2,1,0:T(8,128)(2,1)S(1)} %bitcast.78), channel_id=1, source_target_pairs={{0,30},{1,31},{2,0},{3,1},{4,2},{5,3},{6,4},{7,5},{8,6},{9,7},{10,... | collective-permute-start | bytes 786440 | tf_op jit(solution)/shard_map/ppermute | solution.py:12
  127.6 0.6 collective-permute-start.6
  128.3 3.0 collective-permute-done.4
  131.4 2.8 collective-permute-done.5
  134.2 3.1 collective-permute-done.6
  137.2 2.4 collective-permute-done.7
  139.8 1.0 fusion.18
  140.8 250.7 %all-reduce.3.cloned.1.call-done = (f32[512,512]{0,1:T(8,128)}, f32[512,512]{0,1:T(8,128)}) async-done(((f32[512,512]{0,1:T(8,128)}, f32[512,512]{0,1:T(8,128)}), (f32[512,512]{0,1:T(8,128)}, f32[512,512]{0,1:T(8,128)})) %all-reduce.3.cloned.1.call-update) | async-done | bytes 2097168 | tf_op jit(solution)/shard_map/psum | solution.py:64
  391.5 1.8 broadcast_multiply_fusion
  393.4 1.3 copy.15
  394.7 1.3 copy.16
  (35 shorter events, 1.2 us)
Async XLA Ops:
  7.2 20.8 %copy-start = (bf16[512,512]{1,0:T(8,128)(2,1)S(1)}, bf16[512,512]{1,0:T(8,128)(2,1)}, u32[]{:S(2)}) copy-start(bf16[512,512]{1,0:T(8,128)(2,1)} %param.14) | copy-start | bytes 1572868
  7.2 13.3 %copy-start.2 = (bf16[256,512]{1,0:T(8,128)(2,1)S(1)}, bf16[256,512]{1,0:T(8,128)(2,1)}, u32[]{:S(2)}) copy-start(bf16[256,512]{1,0:T(8,128)(2,1)} %param.9) | copy-start | bytes 786436
  7.2 384.4 %all-reduce.3.cloned.1.call-start = ((), (), s32[]{:S(2)}) async-start(), calls=%async_computation | async-start | bytes 4194304 | tf_op jit(solution)/shard_map/psum | solution.py:64
  7.2 12.1 %collective-permute-start = (bf16[2,128,512]{2,1,0:T(8,128)(2,1)}, bf16[2,128,512]{2,1,0:T(8,128)(2,1)S(1)}, u32[]{:S(2)}, u32[]{:S(2)}) collective-permute-start(bf16[2,128,512]{2,1,0:T(8,128)(2,1)} %bitcast.67), channel_id=1, source_target_pairs={{0,2},{1,3},{2,4},{3,5},{4,6},{5,7},{6,8},{7,9},{8,10},{9,11},{10,... | collective-permute-start | bytes 786440 | tf_op jit(solution)/shard_map/ppermute | solution.py:12
  8.9 11.6 %collective-permute-start.1 = (bf16[2,128,512]{2,1,0:T(8,128)(2,1)}, bf16[2,128,512]{2,1,0:T(8,128)(2,1)S(1)}, u32[]{:S(2)}, u32[]{:S(2)}) collective-permute-start(bf16[2,128,512]{2,1,0:T(8,128)(2,1)} %bitcast.68), channel_id=1, source_target_pairs={{0,1},{1,2},{2,3},{3,4},{4,5},{5,6},{6,7},{7,8},{8,9},{9,10},{10,1... | collective-permute-start | bytes 786440 | tf_op jit(solution)/shard_map/ppermute | solution.py:12
  8.9 11.7 %collective-permute-start.2 = (bf16[2,128,512]{2,1,0:T(8,128)(2,1)}, bf16[2,128,512]{2,1,0:T(8,128)(2,1)S(1)}, u32[]{:S(2)}, u32[]{:S(2)}) collective-permute-start(bf16[2,128,512]{2,1,0:T(8,128)(2,1)} %bitcast.69), channel_id=1, source_target_pairs={{0,31},{1,0},{2,1},{3,2},{4,3},{5,4},{6,5},{7,6},{8,7},{9,8},{10,9... | collective-permute-start | bytes 786440 | tf_op jit(solution)/shard_map/ppermute | solution.py:12
  12.7 9.3 %collective-permute-start.3 = (bf16[2,128,512]{2,1,0:T(8,128)(2,1)}, bf16[2,128,512]{2,1,0:T(8,128)(2,1)S(1)}, u32[]{:S(2)}, u32[]{:S(2)}) collective-permute-start(bf16[2,128,512]{2,1,0:T(8,128)(2,1)} %bitcast.70), channel_id=1, source_target_pairs={{0,30},{1,31},{2,0},{3,1},{4,2},{5,3},{6,4},{7,5},{8,6},{9,7},{10,... | collective-permute-start | bytes 786440 | tf_op jit(solution)/shard_map/ppermute | solution.py:12
  22.0 2.8 copy-start.1
  24.8 3.1 copy-start.4
  24.8 3.1 copy-start.5
  122.5 17.3 %copy-start.3 = (bf16[512,512]{1,0:T(8,128)(2,1)S(1)}, bf16[512,512]{1,0:T(8,128)(2,1)}, u32[]{:S(2)}) copy-start(bf16[512,512]{1,0:T(8,128)(2,1)} %param.13) | copy-start | bytes 1572868
  122.6 8.8 %collective-permute-start.4 = (bf16[2,128,512]{2,1,0:T(8,128)(2,1)S(1)}, bf16[2,128,512]{2,1,0:T(8,128)(2,1)S(1)}, u32[]{:S(2)}, u32[]{:S(2)}) collective-permute-start(bf16[2,128,512]{2,1,0:T(8,128)(2,1)S(1)} %bitcast.78), channel_id=1, source_target_pairs={{0,30},{1,31},{2,0},{3,1},{4,2},{5,3},{6,4},{7,5},{8,6},{9,7},{10,... | collective-permute-start | bytes 786440 | tf_op jit(solution)/shard_map/ppermute | solution.py:12
  127.5 6.7 %collective-permute-start.5 = (bf16[2,128,512]{2,1,0:T(8,128)(2,1)S(1)}, bf16[2,128,512]{2,1,0:T(8,128)(2,1)S(1)}, u32[]{:S(2)}, u32[]{:S(2)}) collective-permute-start(bf16[2,128,512]{2,1,0:T(8,128)(2,1)S(1)} %bitcast.79), channel_id=1, source_target_pairs={{0,31},{1,0},{2,1},{3,2},{4,3},{5,4},{6,5},{7,6},{8,7},{9,8},{10,9... | collective-permute-start | bytes 786440 | tf_op jit(solution)/shard_map/ppermute | solution.py:12
  127.6 9.6 %collective-permute-start.6 = (bf16[2,128,512]{2,1,0:T(8,128)(2,1)S(1)}, bf16[2,128,512]{2,1,0:T(8,128)(2,1)S(1)}, u32[]{:S(2)}, u32[]{:S(2)}) collective-permute-start(bf16[2,128,512]{2,1,0:T(8,128)(2,1)S(1)} %bitcast.80), channel_id=1, source_target_pairs={{0,1},{1,2},{2,3},{3,4},{4,5},{5,6},{6,7},{7,8},{8,9},{9,10},{10,1... | collective-permute-start | bytes 786440 | tf_op jit(solution)/shard_map/ppermute | solution.py:12
  128.2 11.4 %collective-permute-start.7 = (bf16[2,128,512]{2,1,0:T(8,128)(2,1)S(1)}, bf16[2,128,512]{2,1,0:T(8,128)(2,1)S(1)}, u32[]{:S(2)}, u32[]{:S(2)}) collective-permute-start(bf16[2,128,512]{2,1,0:T(8,128)(2,1)S(1)} %bitcast.81), channel_id=1, source_target_pairs={{0,2},{1,3},{2,4},{3,5},{4,6},{5,7},{6,8},{7,9},{8,10},{9,11},{10,... | collective-permute-start | bytes 786440 | tf_op jit(solution)/shard_map/ppermute | solution.py:12
Sparse Core Ops, SparseCore 0:
  121.8 269.6 all-reduce.2
where the time goes:
time: 403 us
  waiting for transfers between devices  265 us (66%)
  other arithmetic  84.4 us (21%)
  local copies, waits for them, and re-layouts  16.1 us (4%)
  between operations  14.2 us (4%)
  matrix products  11.9 us (3%)
  starting transfers between devices  11.6 us (3%)
    psum x1, waiting for transfers between devices, local(): total_self, total_neigh = lax.psum((part_self, part_neigh), ('grp', 'feat'))  251 us
    scatter-add x1, other arithmetic, local(): jax.ops.segment_sum(contrib_flat, flat_index, num_segments=window_count)  75.4 us
    ppermute x8, waiting for transfers between devices, passed_along(): return lax.ppermute(x, axis, [(i, (i + by) % peers) for i in range(peers)])  13.8 us
    ppermute x8, starting transfers between devices, passed_along(): return lax.ppermute(x, axis, [(i, (i + by) % peers) for i in range(peers)])  11.6 us
    unnamed x23, local copies, waits for them, and re-layouts  10.9 us
  transfers between devices with their start and end apart: 9, of which 7 were waited for; matrix products, arithmetic and copies ran while one was open for 2% of the time, Pallas kernels for 0%

commit v1 on v0

--- a/solution.py
+++ b/solution.py
@@ -61,7 +61,7 @@
     ).astype(jnp.bfloat16)
     part_self = jnp.dot(features.T, grad_pre, preferred_element_type=jnp.float32)
     part_neigh = jnp.dot(aggregated.T, grad_pre, preferred_element_type=jnp.float32)
-    total_self, total_neigh = lax.psum((part_self, part_neigh), ("grp", "feat"))
+    total_self, total_neigh = lax.psum(lax.psum((part_self, part_neigh), "grp"), "feat")
     grad_scale = 1.0 / math.sqrt(row_count * lax.axis_size("grp") * feat_count)
     own_part = jnp.dot(grad_pre, w_self.T, preferred_element_type=jnp.float32)
     back = jnp.dot(grad_pre, w_neigh.T, preferred_element_type=jnp.float32).reshape(

time: 403 us -> 259 us (0.64)
  waiting for transfers between devices: 265 us -> 118 us
    psum x1 -> x2, waiting for transfers between devices: 251 us -> 104 us  [the longest x1 104 us: local(): lax.psum(lax.psum((part_self, part_neigh), 'grp'), 'feat')]
  transfers between devices with their start and end apart: 9 -> 10, of which waited for: 7 -> 7; matrix products, arithmetic and copies ran while one was open for 2% -> 38% of each run, Pallas kernels for 0% -> 0%
where the time goes in v1:
time: 259 us; the launch traced here: 257 us
  waiting for transfers between devices  118 us (46%)
  other arithmetic  84.8 us (33%)
  local copies, waits for them, and re-layouts  16.1 us (6%)
  between operations  14.3 us (6%)
  matrix products  11.9 us (5%)
  starting transfers between devices  11.6 us (4%)
    psum x1, waiting for transfers between devices, local(): lax.psum(lax.psum((part_self, part_neigh), 'grp'), 'feat')  104 us
    scatter-add x1, other arithmetic, local(): jax.ops.segment_sum(contrib_flat, flat_index, num_segments=window_count)  75.9 us
    ppermute x8, waiting for transfers between devices, passed_along(): return lax.ppermute(x, axis, [(i, (i + by) % peers) for i in range(peers)])  13.9 us
    ppermute x8, starting transfers between devices, passed_along(): return lax.ppermute(x, axis, [(i, (i + by) % peers) for i in range(peers)])  11.3 us
    unnamed x23, local copies, waits for them, and re-layouts  10.9 us
  transfers between devices with their start and end apart: 10, of which 7 were waited for; matrix products, arithmetic and copies ran while one was open for 38% of the time, Pallas kernels for 0%

profile of v1, /device:TPU:2, one launch (start us, length us, event | category | flops | bytes accessed | tf_op | source)
XLA Modules:
  0.0 257.2 jit_solution(12141913314779163826)
XLA Ops:
  7.2 1.7 collective-permute-start
  8.9 3.9 %collective-permute-start.2 = (bf16[2,128,512]{2,1,0:T(8,128)(2,1)}, bf16[2,128,512]{2,1,0:T(8,128)(2,1)S(1)}, u32[]{:S(2)}, u32[]{:S(2)}) collective-permute-start(bf16[2,128,512]{2,1,0:T(8,128)(2,1)} %bitcast.69), channel_id=1, source_target_pairs={{0,31},{1,0},{2,1},{3,2},{4,3},{5,4},{6,5},{7,6},{8,7},{9,8},{10,9... | collective-permute-start | bytes 786440 | tf_op jit(solution)/shard_map/ppermute | solution.py:12
  12.7 0.4 collective-permute-start.3
  13.2 0.7 compare_and_fusion
  14.0 0.7 iota_compare_fusion
  14.7 2.2 fusion.33
  16.9 0.7 exponential_multiply_fusion
  17.6 1.6 convert_reduce_fusion
  19.3 1.2 collective-permute-done.1
  20.6 1.4 collective-permute-done.3
  22.0 2.8 %gather_fusion = bf16[32,128,512]{2,1,0:T(8,128)(2,1)} fusion(bf16[10,128,512]{2,1,0:T(8,128)(2,1)S(1)} %constant_dynamic-update-slice_fusion, s32[1024]{0:T(1024)S(1)} %pad_clamp_fusion), kind=kCustom, calls=%fused_computation | custom fusion | bytes 8388736 | tf_op jit(solution)/shard_map/jit(_take)/gather | solution.py:46
  24.8 3.1 %fusion.11 = bf16[2,128,512]{2,1,0:T(8,128)(2,1)S(1)} fusion(bf16[2,16,128,512]{3,2,1,0:T(8,128)(2,1)} %bitcast.66, pred[2,16]{1,0:T(4,128)(4,1)S(1)} %get-tuple-element.12, bf16[2,16,128,128]{3,2,1,0:T(8,128)(2,1)S(1)} %copy-done.1, pred[2,16]{1,0:T(4,128)(4,1)S(1)} %iota_compare_fusion, f32[2,128]{1,0:T(2,128)S(1)} %rsqrt.7), kind=kOutput, calls=%fused_computation.12 | convolution fusion | flops 539754496 | bytes 5506112 | tf_op jit(solution)/shard_map/bkij,bkjf->bif/dot_general | solution.py:49
  28.0 1.2 multiply_convert_fusion.1
  29.2 1.3 fusion.35
  30.5 1.3 convolution_bitcast_fusion
  32.5 1.4 fusion.14
  33.9 8.1 %copy.21 = f32[4,8,128,512]{3,1,2,0:T(8,128)} copy(f32[4,8,128,512]{3,2,1,0:T(8,128)S(1)} %bitcast.65) | data formatting | bytes 16777216
  42.0 2.2 broadcast_in_dim.35
  44.2 75.9 %scatter_fusion = f32[10,65536]{1,0:T(8,128)} fusion(f32[10,65536]{1,0:T(8,128)} %broadcast_in_dim.35, s32[32]{0:T(128)S(1)} %reshape.113, f32[32,65536]{1,0:T(8,128)} %bitcast.64), kind=kCustom, calls=%fused_computation.1 | custom fusion | flops 2097152 | bytes 25165952 | tf_op jit(solution)/shard_map/scatter-add | solution.py:74
  120.1 2.4 convert_element_type.52
  122.6 0.8 fusion.32
  123.5 4.6 %collective-permute-start.4 = (bf16[2,128,512]{2,1,0:T(8,128)(2,1)S(1)}, bf16[2,128,512]{2,1,0:T(8,128)(2,1)S(1)}, u32[]{:S(2)}, u32[]{:S(2)}) collective-permute-start(bf16[2,128,512]{2,1,0:T(8,128)(2,1)S(1)} %bitcast.78), channel_id=1, source_target_pairs={{0,30},{1,31},{2,0},{3,1},{4,2},{5,3},{6,4},{7,5},{8,6},{9,7},{10,... | collective-permute-start | bytes 786440 | tf_op jit(solution)/shard_map/ppermute | solution.py:12
  128.2 0.6 collective-permute-start.6
  128.9 3.0 %collective-permute-done.4 = bf16[2,128,512]{2,1,0:T(8,128)(2,1)S(1)} collective-permute-done((bf16[2,128,512]{2,1,0:T(8,128)(2,1)S(1)}, bf16[2,128,512]{2,1,0:T(8,128)(2,1)S(1)}, u32[]{:S(2)}, u32[]{:S(2)}) %collective-permute-start.4) | collective-permute-done | bytes 262176 | tf_op jit(solution)/shard_map/ppermute | solution.py:12
  132.0 2.8 %collective-permute-done.5 = bf16[2,128,512]{2,1,0:T(8,128)(2,1)S(1)} collective-permute-done((bf16[2,128,512]{2,1,0:T(8,128)(2,1)S(1)}, bf16[2,128,512]{2,1,0:T(8,128)(2,1)S(1)}, u32[]{:S(2)}, u32[]{:S(2)}) %collective-permute-start.5) | collective-permute-done | bytes 262176 | tf_op jit(solution)/shard_map/ppermute | solution.py:12
  134.8 3.1 %collective-permute-done.6 = bf16[2,128,512]{2,1,0:T(8,128)(2,1)S(1)} collective-permute-done((bf16[2,128,512]{2,1,0:T(8,128)(2,1)S(1)}, bf16[2,128,512]{2,1,0:T(8,128)(2,1)S(1)}, u32[]{:S(2)}, u32[]{:S(2)}) %collective-permute-start.6) | collective-permute-done | bytes 262176 | tf_op jit(solution)/shard_map/ppermute | solution.py:12
  137.9 2.4 collective-permute-done.7
  140.4 1.0 fusion.18
  141.4 104.5 %all-reduce.5.cloned.1.call-done = (f32[512,512]{0,1:T(8,128)}, f32[512,512]{0,1:T(8,128)}) async-done(((f32[512,512]{0,1:T(8,128)}, f32[512,512]{0,1:T(8,128)}), (f32[512,512]{0,1:T(8,128)}, f32[512,512]{0,1:T(8,128)})) %all-reduce.5.cloned.1.call-update) | async-done | bytes 2097168 | tf_op jit(solution)/shard_map/psum | solution.py:64
  245.9 1.8 broadcast_multiply_fusion
  247.7 1.3 copy.15
  249.1 1.3 copy.16
  (38 shorter events, 1.4 us)
Async XLA Ops:
  7.2 20.8 %copy-start = (bf16[512,512]{1,0:T(8,128)(2,1)S(1)}, bf16[512,512]{1,0:T(8,128)(2,1)}, u32[]{:S(2)}) copy-start(bf16[512,512]{1,0:T(8,128)(2,1)} %param.14) | copy-start | bytes 1572868
  7.2 13.3 %copy-start.2 = (bf16[256,512]{1,0:T(8,128)(2,1)S(1)}, bf16[256,512]{1,0:T(8,128)(2,1)}, u32[]{:S(2)}) copy-start(bf16[256,512]{1,0:T(8,128)(2,1)} %param.9) | copy-start | bytes 786436
  7.2 115.4 %all-reduce.7.cloned.1.call-start = ((), (), s32[]{:S(2)}) async-start(), calls=%async_computation.1 | async-start | bytes 4194304 | tf_op jit(solution)/shard_map/psum | solution.py:64
  7.2 12.0 %collective-permute-start = (bf16[2,128,512]{2,1,0:T(8,128)(2,1)}, bf16[2,128,512]{2,1,0:T(8,128)(2,1)S(1)}, u32[]{:S(2)}, u32[]{:S(2)}) collective-permute-start(bf16[2,128,512]{2,1,0:T(8,128)(2,1)} %bitcast.67), channel_id=1, source_target_pairs={{0,2},{1,3},{2,4},{3,5},{4,6},{5,7},{6,8},{7,9},{8,10},{9,11},{10,... | collective-permute-start | bytes 786440 | tf_op jit(solution)/shard_map/ppermute | solution.py:12
  8.9 11.6 %collective-permute-start.1 = (bf16[2,128,512]{2,1,0:T(8,128)(2,1)}, bf16[2,128,512]{2,1,0:T(8,128)(2,1)S(1)}, u32[]{:S(2)}, u32[]{:S(2)}) collective-permute-start(bf16[2,128,512]{2,1,0:T(8,128)(2,1)} %bitcast.68), channel_id=1, source_target_pairs={{0,1},{1,2},{2,3},{3,4},{4,5},{5,6},{6,7},{7,8},{8,9},{9,10},{10,1... | collective-permute-start | bytes 786440 | tf_op jit(solution)/shard_map/ppermute | solution.py:12
  8.9 11.7 %collective-permute-start.2 = (bf16[2,128,512]{2,1,0:T(8,128)(2,1)}, bf16[2,128,512]{2,1,0:T(8,128)(2,1)S(1)}, u32[]{:S(2)}, u32[]{:S(2)}) collective-permute-start(bf16[2,128,512]{2,1,0:T(8,128)(2,1)} %bitcast.69), channel_id=1, source_target_pairs={{0,31},{1,0},{2,1},{3,2},{4,3},{5,4},{6,5},{7,6},{8,7},{9,8},{10,9... | collective-permute-start | bytes 786440 | tf_op jit(solution)/shard_map/ppermute | solution.py:12
  12.7 9.3 %collective-permute-start.3 = (bf16[2,128,512]{2,1,0:T(8,128)(2,1)}, bf16[2,128,512]{2,1,0:T(8,128)(2,1)S(1)}, u32[]{:S(2)}, u32[]{:S(2)}) collective-permute-start(bf16[2,128,512]{2,1,0:T(8,128)(2,1)} %bitcast.70), channel_id=1, source_target_pairs={{0,30},{1,31},{2,0},{3,1},{4,2},{5,3},{6,4},{7,5},{8,6},{9,7},{10,... | collective-permute-start | bytes 786440 | tf_op jit(solution)/shard_map/ppermute | solution.py:12
  22.0 2.8 %copy-start.1 = (bf16[2,16,128,128]{3,2,1,0:T(8,128)(2,1)S(1)}, bf16[2,16,128,128]{3,2,1,0:T(8,128)(2,1)}, u32[]{:S(2)}) copy-start(bf16[2,16,128,128]{3,2,1,0:T(8,128)(2,1)} %param.10) | copy-start | bytes 3145732
  24.8 3.1 %copy-start.4 = (f32[256,512]{1,0:T(8,128)S(1)}, f32[256,512]{1,0:T(8,128)}, u32[]{:S(2)}) copy-start(f32[256,512]{1,0:T(8,128)} %fusion.33) | copy-start | bytes 1572868
  24.8 3.1 %copy-start.5 = (bf16[256,512]{1,0:T(8,128)(2,1)S(1)}, bf16[256,512]{1,0:T(8,128)(2,1)}, u32[]{:S(2)}) copy-start(bf16[256,512]{1,0:T(8,128)(2,1)} %param.17) | copy-start | bytes 786436
  31.8 214.1 %all-reduce.5.cloned.1.call-start = ((), (), s32[]{:S(2)}) async-start(), calls=%async_computation | async-start | bytes 4194304 | tf_op jit(solution)/shard_map/psum | solution.py:64
  123.4 17.0 %copy-start.3 = (bf16[512,512]{1,0:T(8,128)(2,1)S(1)}, bf16[512,512]{1,0:T(8,128)(2,1)}, u32[]{:S(2)}) copy-start(bf16[512,512]{1,0:T(8,128)(2,1)} %param.13) | copy-start | bytes 1572868
  123.5 8.5 %collective-permute-start.4 = (bf16[2,128,512]{2,1,0:T(8,128)(2,1)S(1)}, bf16[2,128,512]{2,1,0:T(8,128)(2,1)S(1)}, u32[]{:S(2)}, u32[]{:S(2)}) collective-permute-start(bf16[2,128,512]{2,1,0:T(8,128)(2,1)S(1)} %bitcast.78), channel_id=1, source_target_pairs={{0,30},{1,31},{2,0},{3,1},{4,2},{5,3},{6,4},{7,5},{8,6},{9,7},{10,... | collective-permute-start | bytes 786440 | tf_op jit(solution)/shard_map/ppermute | solution.py:12
  128.1 6.7 %collective-permute-start.5 = (bf16[2,128,512]{2,1,0:T(8,128)(2,1)S(1)}, bf16[2,128,512]{2,1,0:T(8,128)(2,1)S(1)}, u32[]{:S(2)}, u32[]{:S(2)}) collective-permute-start(bf16[2,128,512]{2,1,0:T(8,128)(2,1)S(1)} %bitcast.79), channel_id=1, source_target_pairs={{0,31},{1,0},{2,1},{3,2},{4,3},{5,4},{6,5},{7,6},{8,7},{9,8},{10,9... | collective-permute-start | bytes 786440 | tf_op jit(solution)/shard_map/ppermute | solution.py:12
  128.2 9.6 %collective-permute-start.6 = (bf16[2,128,512]{2,1,0:T(8,128)(2,1)S(1)}, bf16[2,128,512]{2,1,0:T(8,128)(2,1)S(1)}, u32[]{:S(2)}, u32[]{:S(2)}) collective-permute-start(bf16[2,128,512]{2,1,0:T(8,128)(2,1)S(1)} %bitcast.80), channel_id=1, source_target_pairs={{0,1},{1,2},{2,3},{3,4},{4,5},{5,6},{6,7},{7,8},{8,9},{9,10},{10,1... | collective-permute-start | bytes 786440 | tf_op jit(solution)/shard_map/ppermute | solution.py:12
  128.9 11.4 %collective-permute-start.7 = (bf16[2,128,512]{2,1,0:T(8,128)(2,1)S(1)}, bf16[2,128,512]{2,1,0:T(8,128)(2,1)S(1)}, u32[]{:S(2)}, u32[]{:S(2)}) collective-permute-start(bf16[2,128,512]{2,1,0:T(8,128)(2,1)S(1)} %bitcast.81), channel_id=1, source_target_pairs={{0,2},{1,3},{2,4},{3,5},{4,6},{5,7},{6,8},{7,9},{8,10},{9,11},{10,... | collective-permute-start | bytes 786440 | tf_op jit(solution)/shard_map/ppermute | solution.py:12
Sparse Core Ops, SparseCore 0:
  31.9 86.4 all-reduce.6
  122.7 123.1 all-reduce.4
